TPU v7x, 128 devices: a whole 4x4x4 slice. The times are simulated.
128 devices in a mesh: gx: 8 (over x, core), gy: 16 (over y, z).
Axes of the slice: x: 4, y: 4, z: 4, core: 2. Of those that a mesh axis runs over, the one named last changes fastest.
Arguments:
- point_coords: float32 [3, 2097152], P(None, ('gx', 'gy')), may hold values from -1 to 1
- strengths: float32 [3, 2097152], P(None, ('gx', 'gy')), may hold values from -0.06 to 0.06
- centers: float32 [3, 2048], replicated, may hold values from 0 to 0.3
- half_widths: float32 [2048], replicated, may hold values from 0.1 to 0.3
- tile_source: int32 [128, 128], P(('gx', 'gy')), may hold values from 0 to 2047, as said below
- tile_target: int32 [128, 128], P(('gx', 'gy')), may hold values from 0 to 2047, as said below
- tile_count: int32 [128], P(('gx', 'gy')), may hold values from 1 to 128, as said below
Outputs:
- velocity: float32 [3, 2097152], P(None, ('gx', 'gy'))
Inputs may be any that keep to these rules, and one draw needn't show every extreme that they name: `tile_source`: cluster c belongs to domain c // 16. Among the first tile_count[d] entries of row d at most 1 name clusters of any one domain, and some domain reaches 1; later entries are valid ids of no interaction. `tile_target`: cluster c belongs to domain c // 16. Among the first tile_count[d] entries of row d at most 1 name clusters of any one domain, and some domain reaches 1; later entries are valid ids of no interaction. `tile_count`: 128 on at least one domain.
All inputs are finite; a program needn't handle non-finite values.
Results may differ from a plain program's by a relative error of at most 0.0001.
Values sent between devices are 32-bit elements; how exact they have to be, the bound alone decides.
No kernel may reach another device: no remote copies, remote signals or barrier semaphores. Data moves between devices by JAX's collectives and lax.ppermute only.
A program may use at most 64 MiB of HBM per device.

v0:
```python
import functools
import math

import jax
import jax.numpy as jnp
import numpy as np
from jax import lax
from jax.experimental import pallas as pl
from jax.experimental.pallas import tpu as pltpu
from jax.sharding import PartitionSpec as P

CL_DEV = 16
PTS = 1024
DEG = 7
TILES_DEV = 128
DOMAINS = 128
NODES = DEG + 1
WIDE = 8
NARROW = 4
AXES = ("gx", "gy")

smoothing_sq = 0.01
biot_factor = -0.07957747154594767

node_values = np.cos(np.pi * np.arange(NODES) / DEG)
node_list = [float(v) for v in node_values.astype(np.float32)]
node_scales = [
    1.0 / math.prod(node_list[a] - node_list[m] for m in range(NODES) if m != a)
    for a in range(NODES)
]


def build_constants():
    nodes = node_values.astype(np.float32)
    lane = np.arange(128)
    table = np.zeros((8, 8, 128), np.float32)
    for group in range(4):
        table[group] = nodes[group + 4 * (lane // 64)][None, :]
    table[4] = nodes[(lane // 8) % 8][None, :]
    table[5] = nodes[lane % 8][None, :]
    table[6] = nodes[:, None]
    table[7, :4] = table[:4, 0]
    return table


CONSTANTS = build_constants()


def split_bf16(value):
    high = value.astype(jnp.bfloat16)
    return high, (value - high.astype(jnp.float32)).astype(jnp.bfloat16)


def lagrange_rows(row, sublane):
    spread = jnp.broadcast_to(row, (NODES, row.shape[1]))
    result = None
    for m in range(NODES):
        factor = jnp.where(sublane == m, node_scales[m], spread - node_list[m])
        result = factor if result is None else result * factor
    return result


def paired_rows(basis_y, basis_z):
    return jnp.concatenate([basis_y[b : b + 1] * basis_z for b in range(NODES)], axis=0)


def split_exactly(value):
    high = value.astype(jnp.bfloat16)
    rest = value - high.astype(jnp.float32)
    middle = rest.astype(jnp.bfloat16)
    return high, middle, (rest - middle.astype(jnp.float32)).astype(jnp.bfloat16)


def message_kernel(count_ref, source_ref, target_ref, center_ref, width_ref, out_ref):
    slot = lax.broadcasted_iota(jnp.int32, (DOMAINS, TILES_DEV), 0)
    lane = lax.broadcasted_iota(jnp.int32, (1, TILES_DEV), 1)
    alive = lane < count_ref[0]
    source = jnp.where(alive, source_ref[...], -1)
    target = jnp.where(alive, target_ref[...], -1)
    from_source = jnp.where(slot == source >> 4, 1.0, 0.0).astype(jnp.bfloat16)
    from_target = jnp.where(slot == target >> 4, 1.0, 0.0).astype(jnp.bfloat16)
    clusters = center_ref.shape[1]
    number = lax.broadcasted_iota(jnp.int32, (clusters, TILES_DEV), 0)
    chosen = jnp.where(number == target, 1.0, 0.0).astype(jnp.bfloat16)
    places = jnp.concatenate([center_ref[...], width_ref[...], jnp.zeros((4, clusters))], axis=0)
    terms = jnp.concatenate(split_exactly(places), axis=0)
    rows = jnp.dot(terms, chosen, preferred_element_type=jnp.float32)
    row = lax.broadcasted_iota(jnp.int32, (24, TILES_DEV), 0)
    local_source = ((source & 15) + 1).astype(jnp.float32)
    local_target = ((target & 15) + 1).astype(jnp.float32)
    rows = jnp.where(row == 4, local_source, rows)
    spread = functools.partial(
        lax.dot_general,
        dimension_numbers=(((1,), (1,)), ((), ())),
        preferred_element_type=jnp.float32,
    )
    out_ref[:, 0:24] = spread(from_source, rows.astype(jnp.bfloat16)) + spread(
        from_target, jnp.where(row == 5, local_target, 0.0).astype(jnp.bfloat16)
    )


def basis_kernel(coord_ref, basis_ref):
    sublane = lax.broadcasted_iota(jnp.int32, (NODES, PTS), 0)

    @pl.loop(0, CL_DEV)
    def _(cluster):
        where = pl.ds(pl.multiple_of(cluster * PTS, PTS), PTS)
        for axis in range(3):
            basis_ref[8 * axis : 8 * axis + 8, where] = lagrange_rows(
                coord_ref[axis : axis + 1, where], sublane
            )


def upward_kernel(domain_ref, width_ref, coord_ref, strength_ref, const_ref, center_ref, all_width_ref, feature_ref, own_ref, same_ref, rows_ref):
    same_ref[...] = const_ref[...]
    domain = domain_ref[0]
    nearby = pl.ds(pl.multiple_of((domain >> 3) * 128, 128), 128)
    places = jnp.concatenate(
        [center_ref[:, nearby], all_width_ref[:, nearby], jnp.zeros((4, 128))], axis=0
    )
    own_ref[...] = pltpu.roll(places, 128 - (domain & 7) * CL_DEV, 1)
    sublane = lax.broadcasted_iota(jnp.int32, (NODES, PTS), 0)
    lane = lax.broadcasted_iota(jnp.int32, (8, 128), 1)

    def one_cluster(cluster, rows):
        where = pl.ds(pl.multiple_of(cluster * PTS, PTS), PTS)
        basis = [lagrange_rows(coord_ref[axis : axis + 1, where], sublane) for axis in range(3)]
        paired = paired_rows(basis[1], basis[2])
        weighted = jnp.concatenate(
            [strength_ref[c : c + 1, where] * basis[0] for c in range(3)], axis=0
        )
        paired_high, paired_low = split_bf16(paired)
        weighted_high, weighted_low = split_bf16(weighted)
        left = jnp.concatenate([weighted_high, weighted_low], axis=0)
        contract = functools.partial(
            lax.dot_general,
            dimension_numbers=(((1,), (1,)), ((), ())),
            preferred_element_type=jnp.float32,
        )
        twice_high = jnp.concatenate([paired_high, paired_high], axis=0)
        twice_low = jnp.concatenate([paired_low, paired_low], axis=0)
        by_high = contract(left, twice_high)
        by_low = contract(weighted_high, twice_low)
        charge = by_high[:24] + by_high[24:] + by_low
        charge = charge * biot_factor
        charges = []
        for c in range(3):
            block = charge[8 * c : 8 * c + 8]
            moved = jnp.concatenate([block[4:], block[:4]], axis=0)
            charges.append(jnp.where(lane < 64, block, moved))
        width = width_ref[domain * CL_DEV + cluster]
        node_x = const_ref[7] * width
        node_y = const_ref[4] * width
        node_z = const_ref[5] * width
        moments = [
            node_y * charges[2] - node_z * charges[1],
            node_z * charges[0] - node_x * charges[2],
            node_x * charges[1] - node_y * charges[0],
        ]
        order = [charges[0], charges[1], charges[2], charges[0], charges[1]] + moments
        for row, value in enumerate(order):
            for group in range(4):
                rows[row : row + 1, 128 * group : 128 * group + 128] = value[group : group + 1]
        high, low = split_bf16(rows[...])
        feature_ref[cluster] = jnp.concatenate([high, low], axis=0)

    @pl.loop(0, CL_DEV, step=2)
    def _(cluster):
        for extra in range(2):
            one_cluster(cluster + extra, rows_ref.at[extra])


def kernel_blocks(width, target_x, square_yz, group_pair, lane_pair):
    highs, lows = [], []
    for lanes in (2 * lane_pair, 2 * lane_pair + 1):
        high_rows, low_rows = [], []
        for group in (2 * group_pair, 2 * group_pair + 1):
            for half in range(2):
                apart_x = target_x[lanes] - width * node_list[group + 4 * half]
                square_x = apart_x * apart_x
                for b in range(0, NODES, 2):
                    pair = []
                    for square in square_yz[b : b + 2]:
                        inverse = lax.rsqrt(square + square_x)
                        pair.append(inverse * inverse * inverse)
                    high, low = split_bf16(jnp.concatenate(pair, axis=0))
                    high_rows.append(high)
                    low_rows.append(low)
        highs.append(jnp.concatenate(high_rows, axis=0))
        lows.append(jnp.concatenate(low_rows, axis=0))
    return jnp.concatenate(highs, axis=1), jnp.concatenate(lows, axis=1)


def tile_kernel(request_ref, own_ref, feature_ref, const_ref, out_ref, order_ref, number_ref, place_ref, number_vmem, place_vmem, semaphore):
    sublane = lax.broadcasted_iota(jnp.int32, (8, 128), 0)
    request = request_ref[...].T
    request = request[0:8] + request[8:16] + request[16:24]
    number_vmem[...] = request.astype(jnp.int32)
    place_vmem[0:8] = request
    place_vmem[8:16] = own_ref[...]
    copies = [
        pltpu.make_async_copy(number_vmem, number_ref, semaphore.at[0]),
        pltpu.make_async_copy(place_vmem, place_ref, semaphore.at[1]),
    ]
    for copy in copies:
        copy.start()
    for copy in copies:
        copy.wait()

    def collect(step, count):
        for extra in range(8):
            peer = step * 8 + extra
            order_ref[count] = peer
            count += (number_ref[4, peer] > 0).astype(jnp.int32)
        return count

    total = lax.fori_loop(0, DOMAINS // 8, collect, 0)
    last = order_ref[jnp.maximum(total - 1, 0)]
    for extra in range(WIDE - 1):
        order_ref[total + extra] = last
    wide = (total + WIDE - NARROW - 1) // WIDE
    narrow = (jnp.maximum(total - wide * WIDE, 0) + NARROW - 1) // NARROW

    def one_tile(peer):
        local_id = number_ref[4, peer] - 1
        source_width = place_ref[11, local_id]
        target_width = place_ref[3, peer]
        shift = [place_ref[axis, peer] - place_ref[8 + axis, local_id] for axis in range(3)]
        target_x = [const_ref[group] * target_width + shift[0] for group in range(4)]
        target_y = const_ref[4] * target_width + shift[1]
        target_z = const_ref[5] * target_width + shift[2]
        apart_z = target_z - const_ref[6] * source_width
        square_z = apart_z * apart_z + smoothing_sq
        square_yz = []
        for b in range(NODES):
            apart_y = target_y - source_width * node_list[b]
            square_yz.append(square_z + apart_y * apart_y)
        feature = feature_ref[local_id]
        for lane_pair in range(2):
            summed = None
            for group_pair in range(2):
                columns = feature[:, 256 * group_pair : 256 * group_pair + 256]
                for block in kernel_blocks(
                    source_width, target_x, square_yz, group_pair, lane_pair
                ):
                    product = jnp.dot(columns, block, preferred_element_type=jnp.float32)
                    summed = product if summed is None else summed + product
            summed = summed[:8] + summed[8:]
            for side in range(2):
                lanes = 2 * lane_pair + side
                block = summed[:, 128 * side : 128 * side + 128]
                first = jnp.where(
                    sublane == 0, target_y, jnp.where(sublane == 1, target_z, target_x[lanes])
                )
                second = jnp.where(
                    sublane == 0, target_z, jnp.where(sublane == 1, target_x[lanes], target_y)
                )
                velocity = (
                    first * pltpu.roll(block, 6, 0)
                    - second * pltpu.roll(block, 7, 0)
                    - pltpu.roll(block, 3, 0)
                )
                for c in range(3):
                    out_ref[peer * 12 + c * 4 + lanes] = velocity[c : c + 1]

    @pl.loop(0, wide)
    def _(step):
        for extra in range(WIDE):
            one_tile(order_ref[step * WIDE + extra])

    @pl.loop(0, narrow)
    def _(step):
        for extra in range(NARROW):
            one_tile(order_ref[wide * WIDE + extra])


def relay_kernel(source_ref, target_ref, in_ref, out_ref):
    slot = lax.broadcasted_iota(jnp.int32, (DOMAINS, TILES_DEV), 0)
    from_source = jnp.where(slot == source_ref[...], 1.0, 0.0).astype(jnp.bfloat16)
    from_target = jnp.where(slot == target_ref[...], 1.0, 0.0).astype(jnp.bfloat16)
    order = lax.dot_general(
        from_target, from_source, (((1,), (1,)), ((), ())), preferred_element_type=jnp.float32
    ).astype(jnp.bfloat16)
    arrived = jnp.dot(
        from_source, jnp.ones((TILES_DEV, 128), jnp.bfloat16), preferred_element_type=jnp.float32
    )
    alive = arrived > 0.5
    for chunk in range(12):
        rows = pl.ds(chunk, DOMAINS, stride=12)
        moved = None
        for term in split_exactly(jnp.where(alive, in_ref[rows, :], 0.0)):
            product = jnp.dot(order, term, preferred_element_type=jnp.float32)
            moved = product if moved is None else moved + product
        out_ref[rows, :] = moved


def downward_kernel(owner_ref, part_ref, basis_ref, out_ref, proxy_ref, held_ref, semaphore):
    owner = owner_ref[:, 5:6].astype(jnp.int32)
    column = lax.broadcasted_iota(jnp.int32, (DOMAINS, CL_DEV), 1)
    assign = (owner == column + 1).astype(jnp.bfloat16)
    gather = functools.partial(
        lax.dot_general,
        dimension_numbers=(((0,), (0,)), ((), ())),
        preferred_element_type=jnp.float32,
    )
    for chunk in range(12):
        high, low = split_bf16(part_ref[pl.ds(chunk, DOMAINS, stride=12), :])
        proxy_ref[chunk * CL_DEV : (chunk + 1) * CL_DEV] = gather(assign, high) + gather(
            assign, low
        )

    def one_cluster(cluster):
        where = pl.ds(cluster * PTS, PTS)
        rows = proxy_ref[pl.ds(cluster, 12, stride=CL_DEV), :]
        near, far = rows[:, :64], rows[:, 64:]
        left = jnp.concatenate(
            [piece[4 * c : 4 * c + 4] for c in range(3) for piece in (near, far)], axis=0
        )
        left_high, left_low = split_bf16(left)
        paired_high, paired_low = split_bf16(
            paired_rows(basis_ref[8:16, where], basis_ref[16:24, where])
        )
        spread = jnp.dot(
            jnp.concatenate([left_high, left_low, left_high], axis=1),
            jnp.concatenate([paired_high, paired_high, paired_low], axis=0),
            preferred_element_type=jnp.float32,
        )
        basis_x = basis_ref[0:8, where]
        for c in range(3):
            held_ref[c : c + 1, where] = jnp.sum(
                spread[8 * c : 8 * c + 8] * basis_x, axis=0, keepdims=True
            )

    copies = []
    for cluster in range(CL_DEV):
        one_cluster(cluster)
        if cluster % 4 == 3:
            where = pl.ds((cluster - 3) * PTS, 4 * PTS)
            copies.append(
                pltpu.make_async_copy(
                    held_ref.at[:, where], out_ref.at[:, where], semaphore.at[cluster // 4]
                )
            )
            copies[-1].start()
    for copy in copies:
        copy.wait()


def in_vmem():
    return pl.BlockSpec(memory_space=pltpu.VMEM)


def in_smem():
    return pl.BlockSpec(memory_space=pltpu.SMEM)


def exchange(value):
    return lax.all_to_all(value, AXES, split_axis=0, concat_axis=0, tiled=True)


def settings(mebibytes):
    return pltpu.CompilerParams(vmem_limit_bytes=mebibytes << 20)


def local(point_coords, strengths, centers, half_widths, tile_source, tile_target, tile_count):
    domain = lax.axis_index(AXES).reshape(1)
    const = jnp.asarray(CONSTANTS)
    message = pl.pallas_call(
        message_kernel,
        out_shape=jax.ShapeDtypeStruct((DOMAINS, 128), jnp.float32),
        in_specs=[in_smem()] + [in_vmem()] * 4,
        out_specs=in_vmem(),
        name="message",
    )(tile_count, tile_source, tile_target, centers, half_widths[None, :])
    received = exchange(message.reshape(DOMAINS, 1, 128)).reshape(DOMAINS, 128)

    features, own_places, kept_const = pl.pallas_call(
        upward_kernel,
        out_shape=(
            jax.ShapeDtypeStruct((CL_DEV, 16, 512), jnp.bfloat16),
            jax.ShapeDtypeStruct((8, 128), jnp.float32),
            jax.ShapeDtypeStruct(const.shape, jnp.float32),
        ),
        in_specs=[in_smem(), in_smem()] + [in_vmem()] * 5,
        out_specs=(in_vmem(), in_vmem(), in_vmem()),
        scratch_shapes=[pltpu.VMEM((2, 8, 512), jnp.float32)],
        compiler_params=settings(8),
        cost_estimate=pl.CostEstimate(flops=10**8, bytes_accessed=10**6, transcendentals=0),
        name="upward",
    )(domain, half_widths, point_coords, strengths, const, centers, half_widths[None, :])

    parts = pl.pallas_call(
        tile_kernel,
        out_shape=jax.ShapeDtypeStruct((DOMAINS * 12, 1, 128), jnp.float32),
        in_specs=[in_vmem()] * 4,
        out_specs=in_vmem(),
        scratch_shapes=[
            pltpu.SMEM((DOMAINS + WIDE,), jnp.int32),
            pltpu.SMEM((8, 128), jnp.int32),
            pltpu.SMEM((16, 128), jnp.float32),
            pltpu.VMEM((8, 128), jnp.int32),
            pltpu.VMEM((16, 128), jnp.float32),
            pltpu.SemaphoreType.DMA((2,)),
        ],
        compiler_params=settings(8),
        name="tiles",
    )(received, own_places, features, kept_const)

    relayed = exchange(parts.reshape(DOMAINS, 1, 1536))
    alive = (jnp.arange(TILES_DEV) < tile_count[0])[None, :]
    source_owners = jnp.where(alive, tile_source >> 4, -1)
    target_owners = jnp.where(alive, tile_target >> 4, -1)
    ordered = pl.pallas_call(
        relay_kernel,
        out_shape=jax.ShapeDtypeStruct((DOMAINS * 12, 128), jnp.float32),
        in_specs=[in_vmem()] * 3,
        out_specs=in_vmem(),
        compiler_params=settings(4),
        name="relay",
    )(source_owners, target_owners, relayed.reshape(DOMAINS * 12, 128))
    arrived = exchange(ordered.reshape(DOMAINS, 1, 1536))

    basis = pl.pallas_call(
        basis_kernel,
        out_shape=jax.ShapeDtypeStruct((24, CL_DEV * PTS), jnp.float32),
        in_specs=[in_vmem()],
        out_specs=in_vmem(),
        compiler_params=settings(8),
        cost_estimate=pl.CostEstimate(flops=10**8, bytes_accessed=2 * 10**6, transcendentals=0),
        name="basis",
    )(point_coords)
    return pl.pallas_call(
        downward_kernel,
        out_shape=jax.ShapeDtypeStruct((3, CL_DEV * PTS), jnp.float32),
        in_specs=[in_vmem(), in_vmem(), in_vmem()],
        out_specs=pl.BlockSpec(memory_space=pl.ANY),
        scratch_shapes=[
            pltpu.VMEM((12 * CL_DEV, 128), jnp.float32),
            pltpu.VMEM((3, CL_DEV * PTS), jnp.float32),
            pltpu.SemaphoreType.DMA((CL_DEV // 4,)),
        ],
        compiler_params=settings(8),
        name="downward",
    )(received, arrived.reshape(DOMAINS * 12, 128), basis)


def solution(mesh):
    return jax.shard_map(
        local,
        mesh=mesh,
        in_specs=(
            P(None, AXES),
            P(None, AXES),
            P(),
            P(),
            P(AXES, None),
            P(AXES, None),
            P(AXES),
        ),
        out_specs=P(None, AXES),
        check_vma=False,
    )
```

profile of v0, /device:TPU:1, one launch (start us, length us, event | category | flops | bytes accessed | tf_op | source)
XLA Modules:
  0.0 97.4 jit_solution(1312037961230553915)
XLA Ops:
  0.7 1.8 %message.1 = f32[128,128]{1,0:T(8,128)} custom-call(s32[1]{0:T(128)} %copy.12.count_ref, s32[1,128]{1,0:T(1,128)} %source_ref.1, s32[1,128]{1,0:T(1,128)} %target_ref.1, f32[3,2048]{1,0:T(4,128)} %center_ref.3, f32[1,2048]{1,0:T(1,128)} %bitcast.16), custom_call_target="tpu_custom_call" | custom-call | tf_op jit(solution)/shard_map/message/pallas_call | solution.py:368
  2.4 11.5 %all-to-all-start = ((f32[128,1,128]{2,1,0:T(1,128)}), f32[128,1,128]{2,1,0:T(1,128)S(1)}, u32[]{:S(2)}, u32[]{:S(2)}) async-start(f32[128,1,128]{2,1,0:T(1,128)} %bitcast.18), calls=%async_computation | async-start | bytes 131072 | tf_op jit(solution)/shard_map/all_to_all | solution.py:358
  13.9 0.0 copy-start
  14.0 0.9 copy-done
  14.9 0.0 copy-start.2
  14.9 0.9 copy-done.2
  15.8 0.0 copy-start.3
  15.9 0.8 copy-done.3
  16.6 0.0 copy-start.4
  16.6 0.7 copy-done.4
  17.3 0.0 copy-start.5
  17.3 0.8 copy-done.5
  18.1 0.0 copy-start.6
  18.1 0.0 copy-start.7
  18.1 4.7 %upward.1 = (bf16[16,16,512]{2,1,0:T(8,128)(2,1)S(1)}, f32[8,128]{1,0:T(8,128)S(1)}, f32[8,8,128]{2,1,0:T(8,128)S(1)}) custom-call(s32[1]{0:T(128)} %bitcast.5.domain_ref, f32[2048]{0:T(1024)S(1)} %copy-done.4, f32[3,16384]{1,0:T(4,128)S(1)} %copy-done, f32[3,16384]{1,0:T(4,128)S(1)} %copy-done.2, f32[8,8,128]{2,1,0:T(8,128)S(1)} %copy-done.5, ...), custom_call_target="tpu_custom_call" | custom-call | flops 100000000 | bytes 1000000 | tf_op jit(solution)/shard_map/upward/pallas_call | solution.py:377
  22.8 0.7 all-to-all-done
  23.5 21.3 %tiles.1 = f32[1536,1,128]{2,1,0:T(1,128)} custom-call(f32[128,128]{1,0:T(8,128)S(1)} %bitcast.14, f32[8,128]{1,0:T(8,128)S(1)} %get-tuple-element.8.own_ref, bf16[16,16,512]{2,1,0:T(8,128)(2,1)S(1)} %get-tuple-element.9.feature_ref, f32[8,8,128]{2,1,0:T(8,128)S(1)} %get-tuple-element.10.const_ref), custom_call_target="tpu_custom_call" | custom-call | tf_op jit(solution)/shard_map/tiles/pallas_call | solution.py:392
  44.8 10.9 %all-to-all-start.1 = ((f32[128,1,1536]{2,1,0:T(1,128)}), f32[128,1,1536]{2,1,0:T(1,128)S(1)}, u32[]{:S(2)}, u32[]{:S(2)}) async-start(f32[128,1,1536]{2,1,0:T(1,128)} %bitcast.6), calls=%async_computation.1 | async-start | bytes 1572864 | tf_op jit(solution)/shard_map/all_to_all | solution.py:358
  55.7 0.0 copy-done.6
  55.7 0.0 copy-done.7
  55.7 16.5 %all-to-all-done.1 = f32[128,1,1536]{2,1,0:T(1,128)S(1)} async-done(((f32[128,1,1536]{2,1,0:T(1,128)}), f32[128,1,1536]{2,1,0:T(1,128)S(1)}, u32[]{:S(2)}, u32[]{:S(2)}) %all-to-all-start.1) | async-done | bytes 786464 | tf_op jit(solution)/shard_map/all_to_all | solution.py:358
  72.1 0.0 copy-start.1
  72.1 1.6 %relay.1 = f32[1536,128]{1,0:T(8,128)} custom-call(s32[1,128]{1,0:T(1,128)S(1)} %get-tuple-element.12.source_ref, s32[1,128]{1,0:T(1,128)S(1)} %get-tuple-element.11.target_ref, f32[1536,128]{1,0:T(8,128)S(1)} %bitcast.12), custom_call_target="tpu_custom_call" | custom-call | tf_op jit(solution)/shard_map/relay/pallas_call | solution.py:413
  73.7 4.3 %all-to-all-start.2 = ((f32[128,1,1536]{2,1,0:T(1,128)}), f32[128,1,1536]{2,1,0:T(1,128)S(1)}, u32[]{:S(2)}, u32[]{:S(2)}) async-start(f32[128,1,1536]{2,1,0:T(1,128)} %bitcast.8), calls=%async_computation.2 | async-start | bytes 1572864 | tf_op jit(solution)/shard_map/all_to_all | solution.py:358
  78.0 0.0 copy-done.1
  78.0 1.3 %basis.1.basis_ref = f32[24,16384]{1,0:T(8,128)S(1)} custom-call(f32[3,16384]{1,0:T(4,128)S(1)} %copy-done.1), custom_call_target="tpu_custom_call" | custom-call | flops 100000000 | bytes 2000000 | tf_op jit(solution)/shard_map/basis/pallas_call | solution.py:423
  79.3 15.3 %all-to-all-done.2 = f32[128,1,1536]{2,1,0:T(1,128)S(1)} async-done(((f32[128,1,1536]{2,1,0:T(1,128)}), f32[128,1,1536]{2,1,0:T(1,128)S(1)}, u32[]{:S(2)}, u32[]{:S(2)}) %all-to-all-start.2) | async-done | bytes 786464 | tf_op jit(solution)/shard_map/all_to_all | solution.py:358
  94.6 2.7 %downward.1 = f32[3,16384]{1,0:T(4,128)} custom-call(f32[128,128]{1,0:T(8,128)S(1)} %bitcast.15, f32[1536,128]{1,0:T(8,128)S(1)} %bitcast.13, f32[24,16384]{1,0:T(8,128)S(1)} %basis.1.basis_ref), custom_call_target="tpu_custom_call" | custom-call | tf_op jit(solution)/shard_map/downward/pallas_call | solution.py:432
  (1 shorter events, 0.0 us)
Async XLA Ops:
  2.4 21.0 %all-to-all-start = ((f32[128,1,128]{2,1,0:T(1,128)}), f32[128,1,128]{2,1,0:T(1,128)S(1)}, u32[]{:S(2)}, u32[]{:S(2)}) async-start(f32[128,1,128]{2,1,0:T(1,128)} %bitcast.18), calls=%async_computation | async-start | bytes 131072 | tf_op jit(solution)/shard_map/all_to_all | solution.py:358
  13.9 1.0 copy-start
  14.9 0.9 copy-start.2
  15.8 0.8 copy-start.3
  16.6 0.7 copy-start.4
  17.3 0.8 copy-start.5
  18.1 37.6 %copy-start.6 = (s32[1,128]{1,0:T(1,128)S(1)}, s32[1,128]{1,0:T(1,128)}, u32[]{:S(2)}) copy-start(s32[1,128]{1,0:T(1,128)} %source_ref.1) | copy-start | bytes 1540
  18.1 37.6 %copy-start.7 = (s32[1,128]{1,0:T(1,128)S(1)}, s32[1,128]{1,0:T(1,128)}, u32[]{:S(2)}) copy-start(s32[1,128]{1,0:T(1,128)} %target_ref.1) | copy-start | bytes 1540
  44.8 27.3 %all-to-all-start.1 = ((f32[128,1,1536]{2,1,0:T(1,128)}), f32[128,1,1536]{2,1,0:T(1,128)S(1)}, u32[]{:S(2)}, u32[]{:S(2)}) async-start(f32[128,1,1536]{2,1,0:T(1,128)} %bitcast.6), calls=%async_computation.1 | async-start | bytes 1572864 | tf_op jit(solution)/shard_map/all_to_all | solution.py:358
  72.1 5.9 %copy-start.1 = (f32[3,16384]{1,0:T(4,128)S(1)}, f32[3,16384]{1,0:T(4,128)}, u32[]{:S(2)}) copy-start(f32[3,16384]{1,0:T(4,128)} %coord_ref.3) | copy-start | bytes 589828
  73.7 20.9 %all-to-all-start.2 = ((f32[128,1,1536]{2,1,0:T(1,128)}), f32[128,1,1536]{2,1,0:T(1,128)S(1)}, u32[]{:S(2)}, u32[]{:S(2)}) async-start(f32[128,1,1536]{2,1,0:T(1,128)} %bitcast.8), calls=%async_computation.2 | async-start | bytes 1572864 | tf_op jit(solution)/shard_map/all_to_all | solution.py:358
where the time goes:
time: 98.2 us; the launch traced here: 97.4 us
  Pallas kernels  33.5 us (34%)
  waiting for transfers between devices  32.4 us (33%)
  starting transfers between devices  26.6 us (27%)
  local copies, waits for them, and re-layouts  4.12 us (4%)
    all_to_all x3, waiting for transfers between devices, exchange(): return lax.all_to_all(value, AXES, split_axis=0, concat_axis=0, tiled=True)  32.4 us
    all_to_all x3, starting transfers between devices, exchange(): return lax.all_to_all(value, AXES, split_axis=0, concat_axis=0, tiled=True)  26.6 us
    pallas_call x1, Pallas kernels, local(): pl.pallas_call(tile_kernel, out_shape=jax.ShapeDtypeStruct((DOMAINS * 12,...  21.3 us
    pallas_call x1, Pallas kernels, local(): pl.pallas_call(upward_kernel, out_shape=(jax.ShapeDtypeStruct((CL_DEV, 16...  4.74 us
    unnamed x16, local copies, waits for them, and re-layouts  4.12 us
    pallas_call x1, Pallas kernels, local(): pl.pallas_call(downward_kernel, out_shape=jax.ShapeDtypeStruct((3, CL_DEV...  2.75 us
  transfers between devices with their start and end apart: 3, of which 3 were waited for; matrix products, arithmetic and copies ran while one was open for 0% of the time, Pallas kernels for 6%

commit v1 on v0

--- a/solution.py
+++ b/solution.py
@@ -71,12 +71,14 @@
     return high, middle, (rest - middle.astype(jnp.float32)).astype(jnp.bfloat16)
 
 
-def message_kernel(count_ref, source_ref, target_ref, center_ref, width_ref, out_ref):
+def message_kernel(count_ref, source_ref, target_ref, center_ref, width_ref, out_ref, owner_ref):
     slot = lax.broadcasted_iota(jnp.int32, (DOMAINS, TILES_DEV), 0)
     lane = lax.broadcasted_iota(jnp.int32, (1, TILES_DEV), 1)
     alive = lane < count_ref[0]
     source = jnp.where(alive, source_ref[...], -1)
     target = jnp.where(alive, target_ref[...], -1)
+    owner_ref[0:1] = source >> 4
+    owner_ref[1:2] = target >> 4
     from_source = jnp.where(slot == source >> 4, 1.0, 0.0).astype(jnp.bfloat16)
     from_target = jnp.where(slot == target >> 4, 1.0, 0.0).astype(jnp.bfloat16)
     clusters = center_ref.shape[1]
@@ -99,19 +101,7 @@
     )
 
 
-def basis_kernel(coord_ref, basis_ref):
-    sublane = lax.broadcasted_iota(jnp.int32, (NODES, PTS), 0)
-
-    @pl.loop(0, CL_DEV)
-    def _(cluster):
-        where = pl.ds(pl.multiple_of(cluster * PTS, PTS), PTS)
-        for axis in range(3):
-            basis_ref[8 * axis : 8 * axis + 8, where] = lagrange_rows(
-                coord_ref[axis : axis + 1, where], sublane
-            )
-
-
-def upward_kernel(domain_ref, width_ref, coord_ref, strength_ref, const_ref, center_ref, all_width_ref, feature_ref, own_ref, same_ref, rows_ref):
+def upward_kernel(domain_ref, width_ref, coord_ref, strength_ref, const_ref, center_ref, all_width_ref, feature_ref, own_ref, same_ref, basis_ref, rows_ref):
     same_ref[...] = const_ref[...]
     domain = domain_ref[0]
     nearby = pl.ds(pl.multiple_of((domain >> 3) * 128, 128), 128)
@@ -125,6 +115,8 @@
     def one_cluster(cluster, rows):
         where = pl.ds(pl.multiple_of(cluster * PTS, PTS), PTS)
         basis = [lagrange_rows(coord_ref[axis : axis + 1, where], sublane) for axis in range(3)]
+        for axis in range(3):
+            basis_ref[8 * axis : 8 * axis + 8, where] = basis[axis]
         paired = paired_rows(basis[1], basis[2])
         weighted = jnp.concatenate(
             [strength_ref[c : c + 1, where] * basis[0] for c in range(3)], axis=0
@@ -274,10 +266,10 @@
             one_tile(order_ref[wide * WIDE + extra])
 
 
-def relay_kernel(source_ref, target_ref, in_ref, out_ref):
+def relay_kernel(owner_ref, in_ref, out_ref):
     slot = lax.broadcasted_iota(jnp.int32, (DOMAINS, TILES_DEV), 0)
-    from_source = jnp.where(slot == source_ref[...], 1.0, 0.0).astype(jnp.bfloat16)
-    from_target = jnp.where(slot == target_ref[...], 1.0, 0.0).astype(jnp.bfloat16)
+    from_source = jnp.where(slot == owner_ref[0:1], 1.0, 0.0).astype(jnp.bfloat16)
+    from_target = jnp.where(slot == owner_ref[1:2], 1.0, 0.0).astype(jnp.bfloat16)
     order = lax.dot_general(
         from_target, from_source, (((1,), (1,)), ((), ())), preferred_element_type=jnp.float32
     ).astype(jnp.bfloat16)
@@ -365,24 +357,28 @@
 def local(point_coords, strengths, centers, half_widths, tile_source, tile_target, tile_count):
     domain = lax.axis_index(AXES).reshape(1)
     const = jnp.asarray(CONSTANTS)
-    message = pl.pallas_call(
+    message, owners = pl.pallas_call(
         message_kernel,
-        out_shape=jax.ShapeDtypeStruct((DOMAINS, 128), jnp.float32),
+        out_shape=(
+            jax.ShapeDtypeStruct((DOMAINS, 128), jnp.float32),
+            jax.ShapeDtypeStruct((2, TILES_DEV), jnp.int32),
+        ),
         in_specs=[in_smem()] + [in_vmem()] * 4,
-        out_specs=in_vmem(),
+        out_specs=(in_vmem(), in_vmem()),
         name="message",
     )(tile_count, tile_source, tile_target, centers, half_widths[None, :])
     received = exchange(message.reshape(DOMAINS, 1, 128)).reshape(DOMAINS, 128)
 
-    features, own_places, kept_const = pl.pallas_call(
+    features, own_places, kept_const, basis = pl.pallas_call(
         upward_kernel,
         out_shape=(
             jax.ShapeDtypeStruct((CL_DEV, 16, 512), jnp.bfloat16),
             jax.ShapeDtypeStruct((8, 128), jnp.float32),
             jax.ShapeDtypeStruct(const.shape, jnp.float32),
+            jax.ShapeDtypeStruct((24, CL_DEV * PTS), jnp.float32),
         ),
         in_specs=[in_smem(), in_smem()] + [in_vmem()] * 5,
-        out_specs=(in_vmem(), in_vmem(), in_vmem()),
+        out_specs=(in_vmem(),) * 4,
         scratch_shapes=[pltpu.VMEM((2, 8, 512), jnp.float32)],
         compiler_params=settings(8),
         cost_estimate=pl.CostEstimate(flops=10**8, bytes_accessed=10**6, transcendentals=0),
@@ -407,28 +403,16 @@
     )(received, own_places, features, kept_const)
 
     relayed = exchange(parts.reshape(DOMAINS, 1, 1536))
-    alive = (jnp.arange(TILES_DEV) < tile_count[0])[None, :]
-    source_owners = jnp.where(alive, tile_source >> 4, -1)
-    target_owners = jnp.where(alive, tile_target >> 4, -1)
     ordered = pl.pallas_call(
         relay_kernel,
         out_shape=jax.ShapeDtypeStruct((DOMAINS * 12, 128), jnp.float32),
-        in_specs=[in_vmem()] * 3,
+        in_specs=[in_vmem()] * 2,
         out_specs=in_vmem(),
         compiler_params=settings(4),
         name="relay",
-    )(source_owners, target_owners, relayed.reshape(DOMAINS * 12, 128))
+    )(owners, relayed.reshape(DOMAINS * 12, 128))
     arrived = exchange(ordered.reshape(DOMAINS, 1, 1536))
 
-    basis = pl.pallas_call(
-        basis_kernel,
-        out_shape=jax.ShapeDtypeStruct((24, CL_DEV * PTS), jnp.float32),
-        in_specs=[in_vmem()],
-        out_specs=in_vmem(),
-        compiler_params=settings(8),
-        cost_estimate=pl.CostEstimate(flops=10**8, bytes_accessed=2 * 10**6, transcendentals=0),
-        name="basis",
-    )(point_coords)
     return pl.pallas_call(
         downward_kernel,
         out_shape=jax.ShapeDtypeStruct((3, CL_DEV * PTS), jnp.float32),

time: 98.2 us -> 95.3 us (0.970); the launches traced: 97.4 us -> 96 us
  blocking collectives: 0 us -> 48.6 us
  waiting for transfers between devices: 32.4 us -> 0.63 us
  starting transfers between devices: 26.6 us -> 11.5 us
  Pallas kernels: 33.5 us -> 30.4 us
    all_to_all x0 -> x2, blocking collectives: none -> 48.6 us  [exchange(): return lax.all_to_all(value, AXES, split_axis=0, concat_axis=0, tiled=True)]
    all_to_all x3 -> x1, waiting for transfers between devices: 32.4 us -> 0.63 us  [exchange(): return lax.all_to_all(value, AXES, split_axis=0, concat_axis=0, tiled=True)]
    all_to_all x3 -> x1, starting transfers between devices: 26.6 us -> 11.5 us  [exchange(): return lax.all_to_all(value, AXES, split_axis=0, concat_axis=0, tiled=True)]
    pallas_call x2 -> x1, Pallas kernels: 3.1 us -> 1.79 us  [local(): pl.pallas_call(message_kernel, out_shape=(jax.ShapeDtypeStruct((DOMAINS,...]
    unnamed x16 -> x12, local copies, waits for them, and re-layouts: 4.12 us -> 4.11 us
  transfers between devices with their start and end apart: 3 -> 1, of which waited for: 3 -> 1; matrix products, arithmetic and copies ran while one was open for 0% -> 0% of each run, Pallas kernels for 6% -> 5%
where the time goes in v1:
time: 95.3 us; the launch traced here: 96 us
  blocking collectives  48.6 us (51%)
  Pallas kernels  30.4 us (32%)
  starting transfers between devices  11.5 us (12%)
  local copies, waits for them, and re-layouts  4.11 us (4%)
    all_to_all x2, blocking collectives, exchange(): return lax.all_to_all(value, AXES, split_axis=0, concat_axis=0, tiled=True)  48.6 us
    pallas_call x1, Pallas kernels, local(): pl.pallas_call(tile_kernel, out_shape=jax.ShapeDtypeStruct((DOMAINS * 12,...  20.5 us
    all_to_all x1, starting transfers between devices, exchange(): return lax.all_to_all(value, AXES, split_axis=0, concat_axis=0, tiled=True)  11.5 us
    pallas_call x1, Pallas kernels, local(): pl.pallas_call(upward_kernel, out_shape=(jax.ShapeDtypeStruct((CL_DEV, 16...  4.76 us
    unnamed x12, local copies, waits for them, and re-layouts  4.11 us
    pallas_call x1, Pallas kernels, local(): pl.pallas_call(downward_kernel, out_shape=jax.ShapeDtypeStruct((3, CL_DEV...  2.75 us
  transfers between devices with their start and end apart: 1, of which 1 were waited for; matrix products, arithmetic and copies ran while one was open for 0% of the time, Pallas kernels for 5%

profile of v1, /device:TPU:1, one launch (start us, length us, event | category | flops | bytes accessed | tf_op | source)
XLA Modules:
  0.0 96.0 jit_solution(11004249632010843192)
XLA Ops:
  0.7 1.8 %message.1 = (f32[128,128]{1,0:T(8,128)}, s32[2,128]{1,0:T(2,128)}) custom-call(s32[1]{0:T(128)S(6)} %copy.12.count_ref, s32[1,128]{1,0:T(1,128)} %source_ref.1, s32[1,128]{1,0:T(1,128)} %target_ref.1, f32[3,2048]{1,0:T(4,128)} %center_ref.3, f32[1,2048]{1,0:T(1,128)} %bitcast.16), custom_call_target="tpu_custom_call" | custom-call | tf_op jit(solution)/shard_map/message/pallas_call | solution.py:360
  2.4 11.5 %all-to-all-start = ((f32[128,1,128]{2,1,0:T(1,128)}), f32[128,1,128]{2,1,0:T(1,128)S(1)}, u32[]{:S(2)}, u32[]{:S(2)}) async-start(f32[128,1,128]{2,1,0:T(1,128)} %bitcast.18), calls=%async_computation | async-start | bytes 131072 | tf_op jit(solution)/shard_map/all_to_all | solution.py:350
  13.9 0.0 copy-start
  14.0 0.9 copy-done
  14.9 0.0 copy-start.1
  14.9 0.9 copy-done.1
  15.8 0.0 copy-start.2
  15.9 0.8 copy-done.2
  16.6 0.0 copy-start.3
  16.6 0.7 copy-done.3
  17.3 0.0 copy-start.4
  17.3 0.8 copy-done.4
  18.1 0.0 copy-start.5
  18.1 4.8 %upward.1 = (bf16[16,16,512]{2,1,0:T(8,128)(2,1)S(1)}, f32[8,128]{1,0:T(8,128)S(1)}, f32[8,8,128]{2,1,0:T(8,128)S(1)}, f32[24,16384]{1,0:T(8,128)S(1)}) custom-call(s32[1]{0:T(128)} %bitcast.4.domain_ref, f32[2048]{0:T(1024)S(1)} %copy-done.3, f32[3,16384]{1,0:T(4,128)S(1)} %copy-done, f32[3,16384]{1,0:T(4,128)S(1)} %copy-done.1, ...), custom_call_target="tpu_custom_call" | custom-call | flops 100000000 | bytes 1000000 | tf_op jit(solution)/shard_map/upward/pallas_call | solution.py:372
  22.8 0.6 all-to-all-done
  23.5 20.5 %tiles.1 = f32[1536,1,128]{2,1,0:T(1,128)S(1)} custom-call(f32[128,128]{1,0:T(8,128)S(1)} %bitcast.14, f32[8,128]{1,0:T(8,128)S(1)} %get-tuple-element.13.own_ref, bf16[16,16,512]{2,1,0:T(8,128)(2,1)S(1)} %get-tuple-element.14.feature_ref, f32[8,8,128]{2,1,0:T(8,128)S(1)} %get-tuple-element.15.const_ref), custom_call_target="tpu_custom_call" | custom-call | tf_op jit(solution)/shard_map/tiles/pallas_call | solution.py:388
  44.0 28.2 %all_to_all.15 = f32[128,1,1536]{2,1,0:T(1,128)S(1)} all-to-all(f32[128,1,1536]{2,1,0:T(1,128)S(1)} %bitcast.10), channel_id=1, replica_groups=mesh['gx'=8,'gy'=16] {'gx','gy'}, dimensions={0} | all-to-all | bytes 1572864 | tf_op jit(solution)/shard_map/all_to_all | solution.py:350
  72.1 0.0 copy-done.5
  72.1 0.6 relay.1
  72.8 20.4 %all_to_all.16 = f32[128,1,1536]{2,1,0:T(1,128)S(1)} all-to-all(f32[128,1,1536]{2,1,0:T(1,128)S(1)} %bitcast.13), channel_id=1, replica_groups=mesh['gx'=8,'gy'=16] {'gx','gy'}, dimensions={0} | all-to-all | bytes 1572864 | tf_op jit(solution)/shard_map/all_to_all | solution.py:350
  93.2 2.8 %downward.1 = f32[3,16384]{1,0:T(4,128)} custom-call(f32[128,128]{1,0:T(8,128)S(1)} %bitcast.15, f32[1536,128]{1,0:T(8,128)S(1)} %bitcast.11, f32[24,16384]{1,0:T(8,128)S(1)} %get-tuple-element.16.basis_ref), custom_call_target="tpu_custom_call" | custom-call | tf_op jit(solution)/shard_map/downward/pallas_call | solution.py:416
Async XLA Ops:
  2.4 21.0 %all-to-all-start = ((f32[128,1,128]{2,1,0:T(1,128)}), f32[128,1,128]{2,1,0:T(1,128)S(1)}, u32[]{:S(2)}, u32[]{:S(2)}) async-start(f32[128,1,128]{2,1,0:T(1,128)} %bitcast.18), calls=%async_computation | async-start | bytes 131072 | tf_op jit(solution)/shard_map/all_to_all | solution.py:350
  13.9 1.0 copy-start
  14.9 0.9 copy-start.1
  15.8 0.8 copy-start.2
  16.6 0.7 copy-start.3
  17.3 0.8 copy-start.4
  18.1 54.1 %copy-start.5 = (s32[2,128]{1,0:T(2,128)S(1)}, s32[2,128]{1,0:T(2,128)}, u32[]{:S(2)}) copy-start(s32[2,128]{1,0:T(2,128)} %get-tuple-element.12.owner_ref) | copy-start | bytes 3076

commit v2 on v1

--- a/solution.py
+++ b/solution.py
@@ -15,8 +15,7 @@
 TILES_DEV = 128
 DOMAINS = 128
 NODES = DEG + 1
-WIDE = 8
-NARROW = 4
+GROUPS = (8, 4, 2, 1)
 AXES = ("gx", "gy")
 
 smoothing_sq = 0.01
@@ -199,19 +198,12 @@
     for copy in copies:
         copy.wait()
 
-    def collect(step, count):
-        for extra in range(8):
-            peer = step * 8 + extra
-            order_ref[count] = peer
-            count += (number_ref[4, peer] > 0).astype(jnp.int32)
-        return count
-
-    total = lax.fori_loop(0, DOMAINS // 8, collect, 0)
-    last = order_ref[jnp.maximum(total - 1, 0)]
-    for extra in range(WIDE - 1):
-        order_ref[total + extra] = last
-    wide = (total + WIDE - NARROW - 1) // WIDE
-    narrow = (jnp.maximum(total - wide * WIDE, 0) + NARROW - 1) // NARROW
+    total = 0
+    for peer in range(DOMAINS):
+        order_ref[total] = peer
+        total += (number_ref[4, peer] > 0).astype(jnp.int32)
+    order_ref[total] = order_ref[jnp.maximum(total - 1, 0)]
+    padded = total + (total % 4 == 3).astype(jnp.int32)
 
     def one_tile(peer):
         local_id = number_ref[4, peer] - 1
@@ -228,6 +220,8 @@
             apart_y = target_y - source_width * node_list[b]
             square_yz.append(square_z + apart_y * apart_y)
         feature = feature_ref[local_id]
+        first_rows = jnp.where(sublane == 0, target_y, target_z)
+        second_rows = jnp.where(sublane == 0, target_z, target_y)
         for lane_pair in range(2):
             summed = None
             for group_pair in range(2):
@@ -241,12 +235,8 @@
             for side in range(2):
                 lanes = 2 * lane_pair + side
                 block = summed[:, 128 * side : 128 * side + 128]
-                first = jnp.where(
-                    sublane == 0, target_y, jnp.where(sublane == 1, target_z, target_x[lanes])
-                )
-                second = jnp.where(
-                    sublane == 0, target_z, jnp.where(sublane == 1, target_x[lanes], target_y)
-                )
+                first = jnp.where(sublane < 2, first_rows, target_x[lanes])
+                second = jnp.where(sublane == 1, target_x[lanes], second_rows)
                 velocity = (
                     first * pltpu.roll(block, 6, 0)
                     - second * pltpu.roll(block, 7, 0)
@@ -255,15 +245,16 @@
                 for c in range(3):
                     out_ref[peer * 12 + c * 4 + lanes] = velocity[c : c + 1]
 
-    @pl.loop(0, wide)
-    def _(step):
-        for extra in range(WIDE):
-            one_tile(order_ref[step * WIDE + extra])
-
-    @pl.loop(0, narrow)
-    def _(step):
-        for extra in range(NARROW):
-            one_tile(order_ref[wide * WIDE + extra])
+    done = 0
+    for size in GROUPS:
+        rounds = (padded - done) // size
+
+        @pl.loop(0, rounds)
+        def _(step):
+            for extra in range(size):
+                one_tile(order_ref[done + step * size + extra])
+
+        done += rounds * size
 
 
 def relay_kernel(owner_ref, in_ref, out_ref):
@@ -391,7 +382,7 @@
         in_specs=[in_vmem()] * 4,
         out_specs=in_vmem(),
         scratch_shapes=[
-            pltpu.SMEM((DOMAINS + WIDE,), jnp.int32),
+            pltpu.SMEM((DOMAINS + 8,), jnp.int32),
             pltpu.SMEM((8, 128), jnp.int32),
             pltpu.SMEM((16, 128), jnp.float32),
             pltpu.VMEM((8, 128), jnp.int32),

time: 95.3 us -> 92.8 us (0.974); the launches traced: 96 us -> 92.4 us
  Pallas kernels: 30.4 us -> 26.7 us
    pallas_call x1, Pallas kernels: 20.5 us -> 16.8 us  [local(): pl.pallas_call(tile_kernel, out_shape=jax.ShapeDtypeStruct((DOMAINS * 12,...]
where the time goes in v2:
time: 92.8 us; the launch traced here: 92.4 us
  blocking collectives  48.8 us (53%)
  Pallas kernels  26.7 us (29%)
  starting transfers between devices  11.5 us (12%)
  local copies, waits for them, and re-layouts  4.11 us (4%)
    all_to_all x2, blocking collectives, exchange(): return lax.all_to_all(value, AXES, split_axis=0, concat_axis=0, tiled=True)  48.8 us
    pallas_call x1, Pallas kernels, local(): pl.pallas_call(tile_kernel, out_shape=jax.ShapeDtypeStruct((DOMAINS * 12,...  16.8 us
    all_to_all x1, starting transfers between devices, exchange(): return lax.all_to_all(value, AXES, split_axis=0, concat_axis=0, tiled=True)  11.5 us
    pallas_call x1, Pallas kernels, local(): pl.pallas_call(upward_kernel, out_shape=(jax.ShapeDtypeStruct((CL_DEV, 16...  4.76 us
    unnamed x12, local copies, waits for them, and re-layouts  4.11 us
    pallas_call x1, Pallas kernels, local(): pl.pallas_call(downward_kernel, out_shape=jax.ShapeDtypeStruct((3, CL_DEV...  2.75 us
  transfers between devices with their start and end apart: 1, of which 1 were waited for; matrix products, arithmetic and copies ran while one was open for 0% of the time, Pallas kernels for 5%

profile of v2, /device:TPU:1, one launch (start us, length us, event | category | flops | bytes accessed | tf_op | source)
XLA Modules:
  0.0 92.4 jit_solution(16590869064380256239)
XLA Ops:
  0.7 1.8 %message.1 = (f32[128,128]{1,0:T(8,128)}, s32[2,128]{1,0:T(2,128)}) custom-call(s32[1]{0:T(128)S(6)} %copy.12.count_ref, s32[1,128]{1,0:T(1,128)} %source_ref.1, s32[1,128]{1,0:T(1,128)} %target_ref.1, f32[3,2048]{1,0:T(4,128)} %center_ref.3, f32[1,2048]{1,0:T(1,128)} %bitcast.16), custom_call_target="tpu_custom_call" | custom-call | tf_op jit(solution)/shard_map/message/pallas_call | solution.py:351
  2.4 11.5 %all-to-all-start = ((f32[128,1,128]{2,1,0:T(1,128)}), f32[128,1,128]{2,1,0:T(1,128)S(1)}, u32[]{:S(2)}, u32[]{:S(2)}) async-start(f32[128,1,128]{2,1,0:T(1,128)} %bitcast.18), calls=%async_computation | async-start | bytes 131072 | tf_op jit(solution)/shard_map/all_to_all | solution.py:341
  13.9 0.0 copy-start
  14.0 0.9 %copy-done = f32[3,16384]{1,0:T(4,128)S(1)} copy-done((f32[3,16384]{1,0:T(4,128)S(1)}, f32[3,16384]{1,0:T(4,128)}, u32[]{:S(2)}) %copy-start) | copy-done | bytes 196632
  14.9 0.0 copy-start.1
  14.9 0.9 %copy-done.1 = f32[3,16384]{1,0:T(4,128)S(1)} copy-done((f32[3,16384]{1,0:T(4,128)S(1)}, f32[3,16384]{1,0:T(4,128)}, u32[]{:S(2)}) %copy-start.1) | copy-done | bytes 196632
  15.8 0.0 copy-start.2
  15.9 0.8 copy-done.2
  16.6 0.0 copy-start.3
  16.6 0.7 copy-done.3
  17.3 0.0 copy-start.4
  17.3 0.8 copy-done.4
  18.1 0.0 copy-start.5
  18.1 4.8 %upward.1 = (bf16[16,16,512]{2,1,0:T(8,128)(2,1)S(1)}, f32[8,128]{1,0:T(8,128)S(1)}, f32[8,8,128]{2,1,0:T(8,128)S(1)}, f32[24,16384]{1,0:T(8,128)S(1)}) custom-call(s32[1]{0:T(128)} %bitcast.4.domain_ref, f32[2048]{0:T(1024)S(1)} %copy-done.3, f32[3,16384]{1,0:T(4,128)S(1)} %copy-done, f32[3,16384]{1,0:T(4,128)S(1)} %copy-done.1, ...), custom_call_target="tpu_custom_call" | custom-call | flops 100000000 | bytes 1000000 | tf_op jit(solution)/shard_map/upward/pallas_call | solution.py:363
  22.8 0.6 all-to-all-done
  23.5 16.8 %tiles.1 = f32[1536,1,128]{2,1,0:T(1,128)S(1)} custom-call(f32[128,128]{1,0:T(8,128)S(1)} %bitcast.14, f32[8,128]{1,0:T(8,128)S(1)} %get-tuple-element.13.own_ref, bf16[16,16,512]{2,1,0:T(8,128)(2,1)S(1)} %get-tuple-element.14.feature_ref, f32[8,8,128]{2,1,0:T(8,128)S(1)} %get-tuple-element.15.const_ref), custom_call_target="tpu_custom_call" | custom-call | tf_op jit(solution)/shard_map/tiles/pallas_call | solution.py:379
  40.2 28.3 %all_to_all.15 = f32[128,1,1536]{2,1,0:T(1,128)S(1)} all-to-all(f32[128,1,1536]{2,1,0:T(1,128)S(1)} %bitcast.10), channel_id=1, replica_groups=mesh['gx'=8,'gy'=16] {'gx','gy'}, dimensions={0} | all-to-all | bytes 1572864 | tf_op jit(solution)/shard_map/all_to_all | solution.py:341
  68.6 0.0 copy-done.5
  68.6 0.6 relay.1
  69.2 20.4 %all_to_all.16 = f32[128,1,1536]{2,1,0:T(1,128)S(1)} all-to-all(f32[128,1,1536]{2,1,0:T(1,128)S(1)} %bitcast.13), channel_id=1, replica_groups=mesh['gx'=8,'gy'=16] {'gx','gy'}, dimensions={0} | all-to-all | bytes 1572864 | tf_op jit(solution)/shard_map/all_to_all | solution.py:341
  89.7 2.8 %downward.1 = f32[3,16384]{1,0:T(4,128)} custom-call(f32[128,128]{1,0:T(8,128)S(1)} %bitcast.15, f32[1536,128]{1,0:T(8,128)S(1)} %bitcast.11, f32[24,16384]{1,0:T(8,128)S(1)} %get-tuple-element.16.basis_ref), custom_call_target="tpu_custom_call" | custom-call | tf_op jit(solution)/shard_map/downward/pallas_call | solution.py:407
Async XLA Ops:
  2.4 21.0 %all-to-all-start = ((f32[128,1,128]{2,1,0:T(1,128)}), f32[128,1,128]{2,1,0:T(1,128)S(1)}, u32[]{:S(2)}, u32[]{:S(2)}) async-start(f32[128,1,128]{2,1,0:T(1,128)} %bitcast.18), calls=%async_computation | async-start | bytes 131072 | tf_op jit(solution)/shard_map/all_to_all | solution.py:341
  13.9 1.0 %copy-start = (f32[3,16384]{1,0:T(4,128)S(1)}, f32[3,16384]{1,0:T(4,128)}, u32[]{:S(2)}) copy-start(f32[3,16384]{1,0:T(4,128)} %coord_ref.1) | copy-start | bytes 589828
  14.9 0.9 %copy-start.1 = (f32[3,16384]{1,0:T(4,128)S(1)}, f32[3,16384]{1,0:T(4,128)}, u32[]{:S(2)}) copy-start(f32[3,16384]{1,0:T(4,128)} %strength_ref.1) | copy-start | bytes 589828
  15.8 0.8 copy-start.2
  16.6 0.7 copy-start.3
  17.3 0.8 copy-start.4
  18.1 50.5 %copy-start.5 = (s32[2,128]{1,0:T(2,128)S(1)}, s32[2,128]{1,0:T(2,128)}, u32[]{:S(2)}) copy-start(s32[2,128]{1,0:T(2,128)} %get-tuple-element.12.owner_ref) | copy-start | bytes 3076

commit v3 on v2

--- a/solution.py
+++ b/solution.py
@@ -15,7 +15,7 @@
 TILES_DEV = 128
 DOMAINS = 128
 NODES = DEG + 1
-GROUPS = (8, 4, 2, 1)
+GROUPS = (16, 8, 4, 2, 1)
 AXES = ("gx", "gy")
 
 smoothing_sq = 0.01

time: 92.8 us -> 91.9 us (level)
  blocking collectives: 48.8 us -> 45 us
  Pallas kernels: 26.7 us -> 29.1 us
    all_to_all x2, blocking collectives: 48.8 us -> 45 us  [exchange(): return lax.all_to_all(value, AXES, split_axis=0, concat_axis=0, tiled=True)]
    pallas_call x1, Pallas kernels: 16.8 us -> 19.1 us  [local(): pl.pallas_call(tile_kernel, out_shape=jax.ShapeDtypeStruct((DOMAINS * 12,...]
where the time goes in v3:
time: 91.9 us; the launch traced here: 91 us
  blocking collectives  45 us (49%)
  Pallas kernels  29.1 us (32%)
  starting transfers between devices  11.5 us (13%)
  local copies, waits for them, and re-layouts  4.11 us (4%)
    all_to_all x2, blocking collectives, exchange(): return lax.all_to_all(value, AXES, split_axis=0, concat_axis=0, tiled=True)  45 us
    pallas_call x1, Pallas kernels, local(): pl.pallas_call(tile_kernel, out_shape=jax.ShapeDtypeStruct((DOMAINS * 12,...  19.1 us
    all_to_all x1, starting transfers between devices, exchange(): return lax.all_to_all(value, AXES, split_axis=0, concat_axis=0, tiled=True)  11.5 us
    pallas_call x1, Pallas kernels, local(): pl.pallas_call(upward_kernel, out_shape=(jax.ShapeDtypeStruct((CL_DEV, 16...  4.76 us
    unnamed x12, local copies, waits for them, and re-layouts  4.11 us
    pallas_call x1, Pallas kernels, local(): pl.pallas_call(downward_kernel, out_shape=jax.ShapeDtypeStruct((3, CL_DEV...  2.75 us
  transfers between devices with their start and end apart: 1, of which 1 were waited for; matrix products, arithmetic and copies ran while one was open for 0% of the time, Pallas kernels for 5%

profile of v3, /device:TPU:1, one launch (start us, length us, event | category | flops | bytes accessed | tf_op | source)
XLA Modules:
  0.0 91.0 jit_solution(16798982452086458580)
XLA Ops:
  0.7 1.8 %message.1 = (f32[128,128]{1,0:T(8,128)}, s32[2,128]{1,0:T(2,128)}) custom-call(s32[1]{0:T(128)S(6)} %copy.12.count_ref, s32[1,128]{1,0:T(1,128)} %source_ref.1, s32[1,128]{1,0:T(1,128)} %target_ref.1, f32[3,2048]{1,0:T(4,128)} %center_ref.3, f32[1,2048]{1,0:T(1,128)} %bitcast.16), custom_call_target="tpu_custom_call" | custom-call | tf_op jit(solution)/shard_map/message/pallas_call | solution.py:351
  2.4 11.5 %all-to-all-start = ((f32[128,1,128]{2,1,0:T(1,128)}), f32[128,1,128]{2,1,0:T(1,128)S(1)}, u32[]{:S(2)}, u32[]{:S(2)}) async-start(f32[128,1,128]{2,1,0:T(1,128)} %bitcast.18), calls=%async_computation | async-start | bytes 131072 | tf_op jit(solution)/shard_map/all_to_all | solution.py:341
  13.9 0.0 copy-start
  14.0 0.9 %copy-done = f32[3,16384]{1,0:T(4,128)S(1)} copy-done((f32[3,16384]{1,0:T(4,128)S(1)}, f32[3,16384]{1,0:T(4,128)}, u32[]{:S(2)}) %copy-start) | copy-done | bytes 196632
  14.9 0.0 copy-start.1
  14.9 0.9 %copy-done.1 = f32[3,16384]{1,0:T(4,128)S(1)} copy-done((f32[3,16384]{1,0:T(4,128)S(1)}, f32[3,16384]{1,0:T(4,128)}, u32[]{:S(2)}) %copy-start.1) | copy-done | bytes 196632
  15.8 0.0 copy-start.2
  15.9 0.8 copy-done.2
  16.6 0.0 copy-start.3
  16.6 0.7 copy-done.3
  17.3 0.0 copy-start.4
  17.3 0.8 copy-done.4
  18.1 0.0 copy-start.5
  18.1 4.8 %upward.1 = (bf16[16,16,512]{2,1,0:T(8,128)(2,1)S(1)}, f32[8,128]{1,0:T(8,128)S(1)}, f32[8,8,128]{2,1,0:T(8,128)S(1)}, f32[24,16384]{1,0:T(8,128)S(1)}) custom-call(s32[1]{0:T(128)} %bitcast.4.domain_ref, f32[2048]{0:T(1024)S(1)} %copy-done.3, f32[3,16384]{1,0:T(4,128)S(1)} %copy-done, f32[3,16384]{1,0:T(4,128)S(1)} %copy-done.1, ...), custom_call_target="tpu_custom_call" | custom-call | flops 100000000 | bytes 1000000 | tf_op jit(solution)/shard_map/upward/pallas_call | solution.py:363
  22.8 0.6 all-to-all-done
  23.5 19.1 %tiles.1 = f32[1536,1,128]{2,1,0:T(1,128)S(1)} custom-call(f32[128,128]{1,0:T(8,128)S(1)} %bitcast.14, f32[8,128]{1,0:T(8,128)S(1)} %get-tuple-element.13.own_ref, bf16[16,16,512]{2,1,0:T(8,128)(2,1)S(1)} %get-tuple-element.14.feature_ref, f32[8,8,128]{2,1,0:T(8,128)S(1)} %get-tuple-element.15.const_ref), custom_call_target="tpu_custom_call" | custom-call | tf_op jit(solution)/shard_map/tiles/pallas_call | solution.py:379
  42.6 24.6 %all_to_all.15 = f32[128,1,1536]{2,1,0:T(1,128)S(1)} all-to-all(f32[128,1,1536]{2,1,0:T(1,128)S(1)} %bitcast.10), channel_id=1, replica_groups=mesh['gx'=8,'gy'=16] {'gx','gy'}, dimensions={0} | all-to-all | bytes 1572864 | tf_op jit(solution)/shard_map/all_to_all | solution.py:341
  67.2 0.0 copy-done.5
  67.2 0.6 relay.1
  67.8 20.4 %all_to_all.16 = f32[128,1,1536]{2,1,0:T(1,128)S(1)} all-to-all(f32[128,1,1536]{2,1,0:T(1,128)S(1)} %bitcast.13), channel_id=1, replica_groups=mesh['gx'=8,'gy'=16] {'gx','gy'}, dimensions={0} | all-to-all | bytes 1572864 | tf_op jit(solution)/shard_map/all_to_all | solution.py:341
  88.2 2.8 %downward.1 = f32[3,16384]{1,0:T(4,128)} custom-call(f32[128,128]{1,0:T(8,128)S(1)} %bitcast.15, f32[1536,128]{1,0:T(8,128)S(1)} %bitcast.11, f32[24,16384]{1,0:T(8,128)S(1)} %get-tuple-element.16.basis_ref), custom_call_target="tpu_custom_call" | custom-call | tf_op jit(solution)/shard_map/downward/pallas_call | solution.py:407
Async XLA Ops:
  2.4 21.0 %all-to-all-start = ((f32[128,1,128]{2,1,0:T(1,128)}), f32[128,1,128]{2,1,0:T(1,128)S(1)}, u32[]{:S(2)}, u32[]{:S(2)}) async-start(f32[128,1,128]{2,1,0:T(1,128)} %bitcast.18), calls=%async_computation | async-start | bytes 131072 | tf_op jit(solution)/shard_map/all_to_all | solution.py:341
  13.9 1.0 %copy-start = (f32[3,16384]{1,0:T(4,128)S(1)}, f32[3,16384]{1,0:T(4,128)}, u32[]{:S(2)}) copy-start(f32[3,16384]{1,0:T(4,128)} %coord_ref.1) | copy-start | bytes 589828
  14.9 0.9 %copy-start.1 = (f32[3,16384]{1,0:T(4,128)S(1)}, f32[3,16384]{1,0:T(4,128)}, u32[]{:S(2)}) copy-start(f32[3,16384]{1,0:T(4,128)} %strength_ref.1) | copy-start | bytes 589828
  15.8 0.8 copy-start.2
  16.6 0.7 copy-start.3
  17.3 0.8 copy-start.4
  18.1 49.1 %copy-start.5 = (s32[2,128]{1,0:T(2,128)S(1)}, s32[2,128]{1,0:T(2,128)}, u32[]{:S(2)}) copy-start(s32[2,128]{1,0:T(2,128)} %get-tuple-element.12.owner_ref) | copy-start | bytes 3076

commit v4 on v3

--- a/solution.py
+++ b/solution.py
@@ -271,7 +271,7 @@
     for chunk in range(12):
         rows = pl.ds(chunk, DOMAINS, stride=12)
         moved = None
-        for term in split_exactly(jnp.where(alive, in_ref[rows, :], 0.0)):
+        for term in split_bf16(jnp.where(alive, in_ref[rows, :], 0.0)):
             product = jnp.dot(order, term, preferred_element_type=jnp.float32)
             moved = product if moved is None else moved + product
         out_ref[rows, :] = moved

time: 91.9 us -> 91.5 us (level)
  no operation moved by 1% of the time
where the time goes in v4:
time: 91.5 us; the launch traced here: 90.8 us
  blocking collectives  45 us (49%)
  Pallas kernels  28.9 us (32%)
  starting transfers between devices  11.5 us (13%)
  local copies, waits for them, and re-layouts  4.11 us (4%)
    all_to_all x2, blocking collectives, exchange(): return lax.all_to_all(value, AXES, split_axis=0, concat_axis=0, tiled=True)  45 us
    pallas_call x1, Pallas kernels, local(): pl.pallas_call(tile_kernel, out_shape=jax.ShapeDtypeStruct((DOMAINS * 12,...  19.1 us
    all_to_all x1, starting transfers between devices, exchange(): return lax.all_to_all(value, AXES, split_axis=0, concat_axis=0, tiled=True)  11.5 us
    pallas_call x1, Pallas kernels, local(): pl.pallas_call(upward_kernel, out_shape=(jax.ShapeDtypeStruct((CL_DEV, 16...  4.76 us
    unnamed x12, local copies, waits for them, and re-layouts  4.11 us
    pallas_call x1, Pallas kernels, local(): pl.pallas_call(downward_kernel, out_shape=jax.ShapeDtypeStruct((3, CL_DEV...  2.75 us
  transfers between devices with their start and end apart: 1, of which 1 were waited for; matrix products, arithmetic and copies ran while one was open for 0% of the time, Pallas kernels for 5%

profile of v4, /device:TPU:1, one launch (start us, length us, event | category | flops | bytes accessed | tf_op | source)
XLA Modules:
  0.0 90.8 jit_solution(6081376065248717506)
XLA Ops:
  0.7 1.8 %message.1 = (f32[128,128]{1,0:T(8,128)}, s32[2,128]{1,0:T(2,128)}) custom-call(s32[1]{0:T(128)S(6)} %copy.12.count_ref, s32[1,128]{1,0:T(1,128)} %source_ref.1, s32[1,128]{1,0:T(1,128)} %target_ref.1, f32[3,2048]{1,0:T(4,128)} %center_ref.3, f32[1,2048]{1,0:T(1,128)} %bitcast.16), custom_call_target="tpu_custom_call" | custom-call | tf_op jit(solution)/shard_map/message/pallas_call | solution.py:351
  2.4 11.5 %all-to-all-start = ((f32[128,1,128]{2,1,0:T(1,128)}), f32[128,1,128]{2,1,0:T(1,128)S(1)}, u32[]{:S(2)}, u32[]{:S(2)}) async-start(f32[128,1,128]{2,1,0:T(1,128)} %bitcast.18), calls=%async_computation | async-start | bytes 131072 | tf_op jit(solution)/shard_map/all_to_all | solution.py:341
  13.9 0.0 copy-start
  14.0 0.9 %copy-done = f32[3,16384]{1,0:T(4,128)S(1)} copy-done((f32[3,16384]{1,0:T(4,128)S(1)}, f32[3,16384]{1,0:T(4,128)}, u32[]{:S(2)}) %copy-start) | copy-done | bytes 196632
  14.9 0.0 copy-start.1
  14.9 0.9 %copy-done.1 = f32[3,16384]{1,0:T(4,128)S(1)} copy-done((f32[3,16384]{1,0:T(4,128)S(1)}, f32[3,16384]{1,0:T(4,128)}, u32[]{:S(2)}) %copy-start.1) | copy-done | bytes 196632
  15.8 0.0 copy-start.2
  15.9 0.8 copy-done.2
  16.6 0.0 copy-start.3
  16.6 0.7 copy-done.3
  17.3 0.0 copy-start.4
  17.3 0.8 copy-done.4
  18.1 0.0 copy-start.5
  18.1 4.8 %upward.1 = (bf16[16,16,512]{2,1,0:T(8,128)(2,1)S(1)}, f32[8,128]{1,0:T(8,128)S(1)}, f32[8,8,128]{2,1,0:T(8,128)S(1)}, f32[24,16384]{1,0:T(8,128)S(1)}) custom-call(s32[1]{0:T(128)} %bitcast.4.domain_ref, f32[2048]{0:T(1024)S(1)} %copy-done.3, f32[3,16384]{1,0:T(4,128)S(1)} %copy-done, f32[3,16384]{1,0:T(4,128)S(1)} %copy-done.1, ...), custom_call_target="tpu_custom_call" | custom-call | flops 100000000 | bytes 1000000 | tf_op jit(solution)/shard_map/upward/pallas_call | solution.py:363
  22.8 0.6 all-to-all-done
  23.5 19.1 %tiles.1 = f32[1536,1,128]{2,1,0:T(1,128)S(1)} custom-call(f32[128,128]{1,0:T(8,128)S(1)} %bitcast.14, f32[8,128]{1,0:T(8,128)S(1)} %get-tuple-element.13.own_ref, bf16[16,16,512]{2,1,0:T(8,128)(2,1)S(1)} %get-tuple-element.14.feature_ref, f32[8,8,128]{2,1,0:T(8,128)S(1)} %get-tuple-element.15.const_ref), custom_call_target="tpu_custom_call" | custom-call | tf_op jit(solution)/shard_map/tiles/pallas_call | solution.py:379
  42.6 24.5 %all_to_all.15 = f32[128,1,1536]{2,1,0:T(1,128)S(1)} all-to-all(f32[128,1,1536]{2,1,0:T(1,128)S(1)} %bitcast.10), channel_id=1, replica_groups=mesh['gx'=8,'gy'=16] {'gx','gy'}, dimensions={0} | all-to-all | bytes 1572864 | tf_op jit(solution)/shard_map/all_to_all | solution.py:341
  67.1 0.0 copy-done.5
  67.1 0.5 relay.1
  67.7 20.4 %all_to_all.16 = f32[128,1,1536]{2,1,0:T(1,128)S(1)} all-to-all(f32[128,1,1536]{2,1,0:T(1,128)S(1)} %bitcast.13), channel_id=1, replica_groups=mesh['gx'=8,'gy'=16] {'gx','gy'}, dimensions={0} | all-to-all | bytes 1572864 | tf_op jit(solution)/shard_map/all_to_all | solution.py:341
  88.1 2.8 %downward.1 = f32[3,16384]{1,0:T(4,128)} custom-call(f32[128,128]{1,0:T(8,128)S(1)} %bitcast.15, f32[1536,128]{1,0:T(8,128)S(1)} %bitcast.11, f32[24,16384]{1,0:T(8,128)S(1)} %get-tuple-element.16.basis_ref), custom_call_target="tpu_custom_call" | custom-call | tf_op jit(solution)/shard_map/downward/pallas_call | solution.py:407
Async XLA Ops:
  2.4 21.0 %all-to-all-start = ((f32[128,1,128]{2,1,0:T(1,128)}), f32[128,1,128]{2,1,0:T(1,128)S(1)}, u32[]{:S(2)}, u32[]{:S(2)}) async-start(f32[128,1,128]{2,1,0:T(1,128)} %bitcast.18), calls=%async_computation | async-start | bytes 131072 | tf_op jit(solution)/shard_map/all_to_all | solution.py:341
  13.9 1.0 %copy-start = (f32[3,16384]{1,0:T(4,128)S(1)}, f32[3,16384]{1,0:T(4,128)}, u32[]{:S(2)}) copy-start(f32[3,16384]{1,0:T(4,128)} %coord_ref.1) | copy-start | bytes 589828
  14.9 0.9 %copy-start.1 = (f32[3,16384]{1,0:T(4,128)S(1)}, f32[3,16384]{1,0:T(4,128)}, u32[]{:S(2)}) copy-start(f32[3,16384]{1,0:T(4,128)} %strength_ref.1) | copy-start | bytes 589828
  15.8 0.8 copy-start.2
  16.6 0.7 copy-start.3
  17.3 0.8 copy-start.4
  18.1 49.1 %copy-start.5 = (s32[2,128]{1,0:T(2,128)S(1)}, s32[2,128]{1,0:T(2,128)}, u32[]{:S(2)}) copy-start(s32[2,128]{1,0:T(2,128)} %get-tuple-element.12.owner_ref) | copy-start | bytes 3076
